TPU v7x, 512 devices: a whole 4x4x16 slice. The times are simulated.
512 devices in a mesh: lag: 64 (over z, y), par: 8 (over x, core).
Axes of the slice: x: 4, y: 4, z: 16, core: 2. Of those that a mesh axis runs over, the one named last changes fastest.
Arguments:
- prior_rows: bfloat16 [64, 512, 16384], P('lag', None, 'par'), may hold values from -0.0625 to 0.0625
- raw_rows: bfloat16 [64, 512, 16384], P('lag', None, 'par'), may hold values from -6 to 6
Outputs:
- diag_zero: float32 [64, 512, 512], P('lag', 'par')
- diag_one: float32 [64, 512, 512], P('lag', 'par')
All inputs are finite; a program needn't handle non-finite values.
Results may differ from a plain program's by a relative error of at most 0.0003.
Values may be sent and summed in bfloat16 or wider, within the bound.
No kernel may reach another device: no remote copies, remote signals or barrier semaphores. Data moves between devices by JAX's collectives and lax.ppermute only.
A program may use at most 64 MiB of HBM per device.

v0:
```python
import jax
import jax.numpy as jnp
from jax import lax
from jax.sharding import PartitionSpec as P


def passed_along(block, axis, distance):
    devices = range(lax.axis_size(axis))
    route = [(i - distance, i) for i in devices if i - distance in devices]
    return lax.ppermute(block, axis, route)


def carried_in(part, axis, combine, identity):
    place = lax.axis_index(axis)
    gathered = lax.all_gather(part, axis)
    state = jnp.zeros_like(part) + jnp.asarray(identity, part.dtype)

    def one(turn, state):
        return combine(state, lax.dynamic_index_in_dim(gathered, turn, 0, False))

    return lax.fori_loop(0, place, one, state)


def add_terms(earlier_term, later_term):
    return earlier_term + later_term


def body(prior_rows, raw_rows):
    incoming = passed_along(raw_rows, "lag", -1)
    following = jnp.concatenate([raw_rows[1:], incoming], axis=0)
    offset_zero = jnp.einsum(
        "lsp,ltp->lst", prior_rows, raw_rows, preferred_element_type=jnp.float32
    )
    offset_one = jnp.einsum(
        "lsp,ltp->lst", prior_rows, following, preferred_element_type=jnp.float32
    )
    stacked = jnp.stack([offset_zero, offset_one], axis=0)
    summed = lax.psum(stacked, "par")
    row_count = summed.shape[2] // lax.axis_size("par")
    shares = lax.dynamic_slice_in_dim(summed, lax.axis_index("par") * row_count, row_count, 2)
    running = jnp.cumsum(shares, axis=1)
    totals = running[:, -1]
    earlier = carried_in(totals, "lag", add_terms, jnp.zeros_like(totals))
    result = running + earlier[:, None]
    return (result[0], result[1])


def solution(mesh):
    in_specs = (P("lag", None, "par"), P("lag", None, "par"))
    out_specs = (P("lag", "par", None), P("lag", "par", None))
    return jax.shard_map(body, mesh=mesh, in_specs=in_specs, out_specs=out_specs, check_vma=False)
```

profile of v0, /device:TPU:504, one launch (start us, length us, event | category | flops | bytes accessed | tf_op | source)
XLA Modules:
  0.0 406.9 jit_solution(13441115809973751010)
XLA Ops:
  7.2 2.9 collective-permute-start
  10.2 2.9 fusion.6
  13.0 42.2 %collective-permute-done = bf16[1,512,2048]{2,1,0:T(8,128)(2,1)S(1)} collective-permute-done((bf16[1,512,2048]{2,1,0:T(8,128)(2,1)}, bf16[1,512,2048]{2,1,0:T(8,128)(2,1)S(1)}, u32[]{:S(2)}, u32[]{:S(2)}) %collective-permute-start) | collective-permute-done | bytes 2097184 | tf_op jit(solution)/shard_map/ppermute | solution.py:10
  55.2 1.3 fusion.11
  56.5 1.5 pad_maximum_fusion
  58.1 83.5 %all-reduce.2.cloned.1.call-done = f32[2,1,512,512]{3,2,1,0:T(8,128)} async-done(((f32[2,1,512,512]{3,2,1,0:T(8,128)}), f32[2,1,512,512]{3,2,1,0:T(8,128)}) %all-reduce.2.cloned.1.call-update) | async-done | bytes 2097168 | tf_op jit(solution)/shard_map/psum | solution.py:38
  141.5 1.7 constant_dynamic-slice_fusion
  143.2 189.3 %all-gather.3.cloned.1.call-done = f32[128,1,64,512]{3,2,1,0:T(8,128)} async-done(((f32[2,1,64,512]{3,2,1,0:T(8,128)}), f32[128,1,64,512]{3,2,1,0:T(8,128)}) %all-gather.3.cloned.1.call-update) | async-done | bytes 16777232 | tf_op jit(solution)/shard_map/all_gather | solution.py:15
  332.6 65.8 %while.10 = (s32[]{:T(128)}, f32[2,64,512]{2,1,0:T(8,128)S(1)}, s32[]{:T(128)}, f32[64,2,64,512]{3,2,1,0:T(8,128)}, s32[]{:T(128)}, /*index=5*/s32[]{:T(128)}, s32[]{:T(128)}) while((s32[]{:T(128)}, f32[2,64,512]{2,1,0:T(8,128)S(1)}, s32[]{:T(128)}, f32[64,2,64,512]{3,2,1,0:T(8,128)}, s32[]{:T(128)}, /*index=5*/s32[]{:T(128)}, s32[]{:T(128)}) %tuple.30), condition=%wide.region_2.3_spmd, body=%wide.region_1.0_spmd.sunk | while | flops 65541 | bytes 786555 | solution.py:21
  332.6 1.0 bitcast_add_fusion.3
  333.6 1.0 bitcast_add_fusion.3
  334.7 1.0 bitcast_add_fusion.3
  335.7 1.0 bitcast_add_fusion.3
  336.8 1.0 bitcast_add_fusion.3
  337.8 1.0 bitcast_add_fusion.3
  338.9 1.0 bitcast_add_fusion.3
  339.9 1.0 bitcast_add_fusion.3
  340.9 1.0 bitcast_add_fusion.3
  342.0 1.0 bitcast_add_fusion.3
  343.0 1.0 bitcast_add_fusion.3
  344.1 1.0 bitcast_add_fusion.3
  345.1 1.0 bitcast_add_fusion.3
  346.2 1.0 bitcast_add_fusion.3
  347.2 1.0 bitcast_add_fusion.3
  348.3 1.0 bitcast_add_fusion.3
  349.3 1.0 bitcast_add_fusion.3
  350.3 1.0 bitcast_add_fusion.3
  351.4 1.0 bitcast_add_fusion.3
  352.4 1.0 bitcast_add_fusion.3
  353.5 1.0 bitcast_add_fusion.3
  354.5 1.0 bitcast_add_fusion.3
  355.6 1.0 bitcast_add_fusion.3
  356.6 1.0 bitcast_add_fusion.3
  357.7 1.0 bitcast_add_fusion.3
  358.7 1.0 bitcast_add_fusion.3
  359.7 1.0 bitcast_add_fusion.3
  360.8 1.0 bitcast_add_fusion.3
  361.8 1.0 bitcast_add_fusion.3
  362.9 1.0 bitcast_add_fusion.3
  363.9 1.0 bitcast_add_fusion.3
  365.0 1.0 bitcast_add_fusion.3
  366.0 1.0 bitcast_add_fusion.3
  367.1 1.0 bitcast_add_fusion.3
  368.1 1.0 bitcast_add_fusion.3
  369.1 1.0 bitcast_add_fusion.3
  370.2 1.0 bitcast_add_fusion.3
  371.2 1.0 bitcast_add_fusion.3
  372.3 1.0 bitcast_add_fusion.3
  373.3 1.0 bitcast_add_fusion.3
  374.4 1.0 bitcast_add_fusion.3
  375.4 1.0 bitcast_add_fusion.3
  376.5 1.0 bitcast_add_fusion.3
  377.5 1.0 bitcast_add_fusion.3
  378.5 1.0 bitcast_add_fusion.3
  379.6 1.0 bitcast_add_fusion.3
  380.6 1.0 bitcast_add_fusion.3
  381.7 1.0 bitcast_add_fusion.3
  382.7 1.0 bitcast_add_fusion.3
  383.8 1.0 bitcast_add_fusion.3
  384.8 1.0 bitcast_add_fusion.3
  386.9 1.0 bitcast_add_fusion.3
  389.0 1.0 bitcast_add_fusion.3
  391.1 1.0 bitcast_add_fusion.3
  393.2 1.0 bitcast_add_fusion.3
  (17 shorter events, 10.0 us)
Async XLA Ops:
  7.2 3.0 copy-start
  7.2 134.4 %all-reduce.2.cloned.1.call-start = ((), (), s32[]{:S(2)}) async-start(), calls=%async_computation | async-start | bytes 4194304 | tf_op jit(solution)/shard_map/psum | solution.py:38
  7.2 48.0 %collective-permute-start = (bf16[1,512,2048]{2,1,0:T(8,128)(2,1)}, bf16[1,512,2048]{2,1,0:T(8,128)(2,1)S(1)}, u32[]{:S(2)}, u32[]{:S(2)}) collective-permute-start(bf16[1,512,2048]{2,1,0:T(8,128)(2,1)} %param.5), channel_id=1, source_target_pairs={{8,0},{16,8},{24,16},{32,24},{40,32},{48,40},{56,48},{64,56},{72,6... | collective-permute-start | bytes 6291464 | tf_op jit(solution)/shard_map/ppermute | solution.py:10
  58.0 274.5 %all-gather.3.cloned.1.call-start = ((), (), s32[]{:S(2)}) async-start(), calls=%async_computation.1 | async-start | bytes 17039360 | tf_op jit(solution)/shard_map/all_gather | solution.py:15
Sparse Core Ops, SparseCore 0:
  58.2 83.3 all-reduce.1
  144.5 188.0 all-gather.2
where the time goes:
time: 409 us; the launch traced here: 407 us
  waiting for transfers between devices  315 us (77%)
  other arithmetic  66.9 us (16%)
  between operations  14.1 us (3%)
  matrix products  4.16 us (1%)
    all_gather x1, waiting for transfers between devices, carried_in(): gathered = lax.all_gather(part, axis)  189 us
    psum x1, waiting for transfers between devices, body(): summed = lax.psum(stacked, 'par')  83.5 us
    add x63, other arithmetic, add_terms(): return earlier_term + later_term  64.4 us
    ppermute x1, waiting for transfers between devices, passed_along(): return lax.ppermute(block, axis, route)  42.2 us
  transfers between devices with their start and end apart: 3, of which 3 were waited for; matrix products, arithmetic and copies ran while one was open for 1% of the time, Pallas kernels for 0%

commit v1 on v0

--- a/solution.py
+++ b/solution.py
@@ -35,7 +35,9 @@
         "lsp,ltp->lst", prior_rows, following, preferred_element_type=jnp.float32
     )
     stacked = jnp.stack([offset_zero, offset_one], axis=0)
-    summed = lax.psum(stacked, "par")
+    summed = stacked
+    for hop in (1, 2, 4):
+        summed = summed + lax.ppermute(summed, "par", [(dev, dev ^ hop) for dev in range(8)])
     row_count = summed.shape[2] // lax.axis_size("par")
     shares = lax.dynamic_slice_in_dim(summed, lax.axis_index("par") * row_count, row_count, 2)
     running = jnp.cumsum(shares, axis=1)

time: 409 us -> 434 us (1.061)
  waiting for transfers between devices: 315 us -> 329 us
  starting transfers between devices: 2.99 us -> 13.2 us
    ppermute x0 -> x3, waiting for transfers between devices: none -> 95.9 us  [body(): lax.ppermute(summed, 'par', [(dev, dev ^ hop) for dev in range(8)])]
    psum x1 -> x0, waiting for transfers between devices: 83.5 us -> none  [body(): summed = lax.psum(stacked, 'par')]
    ppermute x0 -> x3, starting transfers between devices: none -> 10.3 us  [body(): lax.ppermute(summed, 'par', [(dev, dev ^ hop) for dev in range(8)])]
    add x0 -> x3, other arithmetic: none -> 4.34 us  [body(): summed + lax.ppermute(summed, 'par', [(dev, dev ^ hop) for dev in range(8)])]
  transfers between devices with their start and end apart: 3 -> 5, of which waited for: 3 -> 5; matrix products, arithmetic and copies ran while one was open for 1% -> 1% of each run, Pallas kernels for 0% -> 0%
where the time goes in v1:
time: 434 us; the launch traced here: 431 us
  waiting for transfers between devices  329 us (76%)
  other arithmetic  69 us (16%)
  between operations  14.1 us (3%)
  starting transfers between devices  13.2 us (3%)
    all_gather x1, waiting for transfers between devices, carried_in(): gathered = lax.all_gather(part, axis)  191 us
    ppermute x3, waiting for transfers between devices, body(): lax.ppermute(summed, 'par', [(dev, dev ^ hop) for dev in range(8)])  95.9 us
    add x63, other arithmetic, add_terms(): return earlier_term + later_term  64.4 us
    ppermute x1, waiting for transfers between devices, passed_along(): return lax.ppermute(block, axis, route)  42.2 us
    ppermute x3, starting transfers between devices, body(): lax.ppermute(summed, 'par', [(dev, dev ^ hop) for dev in range(8)])  10.3 us
  transfers between devices with their start and end apart: 5, of which 5 were waited for; matrix products, arithmetic and copies ran while one was open for 1% of the time, Pallas kernels for 0%

profile of v1, /device:TPU:504, one launch (start us, length us, event | category | flops | bytes accessed | tf_op | source)
XLA Modules:
  0.0 431.4 jit_solution(296833538035204137)
XLA Ops:
  7.2 2.9 collective-permute-start
  10.2 2.9 fusion.6
  13.0 42.2 %collective-permute-done = bf16[1,512,2048]{2,1,0:T(8,128)(2,1)S(1)} collective-permute-done((bf16[1,512,2048]{2,1,0:T(8,128)(2,1)}, bf16[1,512,2048]{2,1,0:T(8,128)(2,1)S(1)}, u32[]{:S(2)}, u32[]{:S(2)}) %collective-permute-start) | collective-permute-done | bytes 2097184 | tf_op jit(solution)/shard_map/ppermute | solution.py:10
  55.2 1.3 fusion.11
  56.7 1.9 collective-permute-start.1
  58.6 4.1 collective-permute-done.1
  63.2 3.4 collective-permute-start.2
  66.6 46.1 %collective-permute-done.2 = f32[2,1,512,512]{3,2,1,0:T(8,128)S(1)} collective-permute-done((f32[2,1,512,512]{3,2,1,0:T(8,128)S(1)}, f32[2,1,512,512]{3,2,1,0:T(8,128)S(1)}, u32[]{:S(2)}, u32[]{:S(2)}) %collective-permute-start.2) | collective-permute-done | bytes 2097184 | tf_op jit(solution)/shard_map/ppermute | solution.py:40
  112.8 2.1 fusion.17
  114.9 4.9 %collective-permute-start.3 = (f32[2,1,512,512]{3,2,1,0:T(8,128)}, f32[2,1,512,512]{3,2,1,0:T(8,128)}, u32[]{:S(2)}, u32[]{:S(2)}) collective-permute-start(f32[2,1,512,512]{3,2,1,0:T(8,128)} %fusion.17), channel_id=1, source_target_pairs={{0,4},{1,5},{2,6},{3,7},{4,0},{5,1},{6,2},{7,3},{8,12},{9,13},{10,... | collective-permute-start | bytes 6291464 | tf_op jit(solution)/shard_map/ppermute | solution.py:40
  119.8 45.6 %collective-permute-done.3 = f32[2,1,512,512]{3,2,1,0:T(8,128)} collective-permute-done((f32[2,1,512,512]{3,2,1,0:T(8,128)}, f32[2,1,512,512]{3,2,1,0:T(8,128)}, u32[]{:S(2)}, u32[]{:S(2)}) %collective-permute-start.3) | collective-permute-done | bytes 2097184 | tf_op jit(solution)/shard_map/ppermute | solution.py:40
  165.4 1.8 dynamic-slice_add_fusion
  167.2 190.8 %all-gather.3.cloned.1.call-done = f32[128,1,64,512]{3,2,1,0:T(8,128)} async-done(((f32[2,1,64,512]{3,2,1,0:T(8,128)}), f32[128,1,64,512]{3,2,1,0:T(8,128)}) %all-gather.3.cloned.1.call-update) | async-done | bytes 16777232 | tf_op jit(solution)/shard_map/all_gather | solution.py:15
  358.0 65.8 %while.10 = (s32[]{:T(128)}, f32[2,64,512]{2,1,0:T(8,128)S(1)}, s32[]{:T(128)}, f32[64,2,64,512]{3,2,1,0:T(8,128)}, s32[]{:T(128)}, /*index=5*/s32[]{:T(128)}, s32[]{:T(128)}) while((s32[]{:T(128)}, f32[2,64,512]{2,1,0:T(8,128)S(1)}, s32[]{:T(128)}, f32[64,2,64,512]{3,2,1,0:T(8,128)}, s32[]{:T(128)}, /*index=5*/s32[]{:T(128)}, s32[]{:T(128)}) %tuple.28), condition=%wide.region_1.2_spmd, body=%wide.region_0.0_spmd.sunk | while | flops 65541 | bytes 786555 | solution.py:21
  358.0 1.1 bitcast_add_fusion.3
  359.1 1.0 bitcast_add_fusion.3
  360.1 1.0 bitcast_add_fusion.3
  361.2 1.0 bitcast_add_fusion.3
  362.2 1.0 bitcast_add_fusion.3
  363.3 1.0 bitcast_add_fusion.3
  364.3 1.0 bitcast_add_fusion.3
  365.4 1.0 bitcast_add_fusion.3
  366.4 1.0 bitcast_add_fusion.3
  367.5 1.0 bitcast_add_fusion.3
  368.5 1.0 bitcast_add_fusion.3
  369.5 1.0 bitcast_add_fusion.3
  370.6 1.0 bitcast_add_fusion.3
  371.6 1.0 bitcast_add_fusion.3
  372.7 1.0 bitcast_add_fusion.3
  373.7 1.0 bitcast_add_fusion.3
  374.8 1.0 bitcast_add_fusion.3
  375.8 1.0 bitcast_add_fusion.3
  376.9 1.0 bitcast_add_fusion.3
  377.9 1.0 bitcast_add_fusion.3
  378.9 1.0 bitcast_add_fusion.3
  380.0 1.0 bitcast_add_fusion.3
  381.0 1.0 bitcast_add_fusion.3
  382.1 1.0 bitcast_add_fusion.3
  383.1 1.0 bitcast_add_fusion.3
  384.2 1.0 bitcast_add_fusion.3
  385.2 1.0 bitcast_add_fusion.3
  386.3 1.0 bitcast_add_fusion.3
  387.3 1.0 bitcast_add_fusion.3
  388.3 1.0 bitcast_add_fusion.3
  389.4 1.0 bitcast_add_fusion.3
  390.4 1.0 bitcast_add_fusion.3
  391.5 1.0 bitcast_add_fusion.3
  392.5 1.0 bitcast_add_fusion.3
  393.6 1.0 bitcast_add_fusion.3
  394.6 1.0 bitcast_add_fusion.3
  395.6 1.0 bitcast_add_fusion.3
  396.7 1.0 bitcast_add_fusion.3
  397.7 1.0 bitcast_add_fusion.3
  398.8 1.0 bitcast_add_fusion.3
  399.8 1.0 bitcast_add_fusion.3
  400.9 1.0 bitcast_add_fusion.3
  401.9 1.0 bitcast_add_fusion.3
  403.0 1.0 bitcast_add_fusion.3
  404.0 1.0 bitcast_add_fusion.3
  405.0 1.0 bitcast_add_fusion.3
  406.1 1.0 bitcast_add_fusion.3
  408.2 1.0 bitcast_add_fusion.3
  410.3 1.0 bitcast_add_fusion.3
  421.8 1.0 bitcast_add_fusion.3
  (24 shorter events, 14.8 us)
Async XLA Ops:
  7.2 3.0 copy-start
  7.2 350.8 %all-gather.3.cloned.1.call-start = ((), (), s32[]{:S(2)}) async-start(), calls=%async_computation | async-start | bytes 17039360 | tf_op jit(solution)/shard_map/all_gather | solution.py:15
  7.2 48.0 %collective-permute-start = (bf16[1,512,2048]{2,1,0:T(8,128)(2,1)}, bf16[1,512,2048]{2,1,0:T(8,128)(2,1)S(1)}, u32[]{:S(2)}, u32[]{:S(2)}) collective-permute-start(bf16[1,512,2048]{2,1,0:T(8,128)(2,1)} %param.5), channel_id=1, source_target_pairs={{8,0},{16,8},{24,16},{32,24},{40,32},{48,40},{56,48},{64,56},{72,6... | collective-permute-start | bytes 6291464 | tf_op jit(solution)/shard_map/ppermute | solution.py:10
  56.7 6.1 %collective-permute-start.1 = (f32[2,1,512,512]{3,2,1,0:T(8,128)S(1)}, f32[2,1,512,512]{3,2,1,0:T(8,128)S(1)}, u32[]{:S(2)}, u32[]{:S(2)}) collective-permute-start(f32[2,1,512,512]{3,2,1,0:T(8,128)S(1)} %pad_maximum_fusion), channel_id=1, source_target_pairs={{0,1},{1,0},{2,3},{3,2},{4,5},{5,4},{6,7},{7,6},{8,9},{9,8},{10,11... | collective-permute-start | bytes 6291464 | tf_op jit(solution)/shard_map/ppermute | solution.py:40
  63.2 49.6 %collective-permute-start.2 = (f32[2,1,512,512]{3,2,1,0:T(8,128)S(1)}, f32[2,1,512,512]{3,2,1,0:T(8,128)S(1)}, u32[]{:S(2)}, u32[]{:S(2)}) collective-permute-start(f32[2,1,512,512]{3,2,1,0:T(8,128)S(1)} %fusion.16), channel_id=1, source_target_pairs={{0,2},{1,3},{2,0},{3,1},{4,6},{5,7},{6,4},{7,5},{8,10},{9,11},{10,... | collective-permute-start | bytes 6291464 | tf_op jit(solution)/shard_map/ppermute | solution.py:40
  114.9 50.5 %collective-permute-start.3 = (f32[2,1,512,512]{3,2,1,0:T(8,128)}, f32[2,1,512,512]{3,2,1,0:T(8,128)}, u32[]{:S(2)}, u32[]{:S(2)}) collective-permute-start(f32[2,1,512,512]{3,2,1,0:T(8,128)} %fusion.17), channel_id=1, source_target_pairs={{0,4},{1,5},{2,6},{3,7},{4,0},{5,1},{6,2},{7,3},{8,12},{9,13},{10,... | collective-permute-start | bytes 6291464 | tf_op jit(solution)/shard_map/ppermute | solution.py:40
  358.0 65.8 %copy-start.1 = (f32[2,1,64,512]{3,2,1,0:T(8,128)S(1)}, f32[2,1,64,512]{3,2,1,0:T(8,128)}, u32[]{:S(2)}) copy-start(f32[2,1,64,512]{3,2,1,0:T(8,128)} %dynamic-slice_add_fusion) | copy-start | bytes 786436
Sparse Core Ops, SparseCore 0:
  167.3 190.6 all-gather.2
